TPU v7x, 32 devices: a whole 2x2x4 slice. The times are simulated.
32 devices in a mesh: region: 4 (over z), tok: 8 (over y, x, core).
Axes of the slice: x: 2, y: 2, z: 4, core: 2. Of those that a mesh axis runs over, the one named last changes fastest.
Arguments:
- tokens: bfloat16 [4096, 1024], P(('region', 'tok')), may hold values from -6 to 6
- w_query: bfloat16 [1024, 1024], P('tok'), may hold values from -0.1875 to 0.1875
- w_key: bfloat16 [1024, 1024], P('tok'), may hold values from -0.1875 to 0.1875
- w_value: bfloat16 [1024, 1024], P('tok'), may hold values from -0.1875 to 0.1875
- w_out: bfloat16 [1024, 1024], P(None, 'tok'), may hold values from -0.1875 to 0.1875
- past_keys: bfloat16 [4, 4096, 1024], P(None, ('region', 'tok')), may hold values from -600 to 600
- past_values: bfloat16 [4, 4096, 1024], P(None, ('region', 'tok')), may hold values from -6 to 6
- nb_block: int32 [32, 8], replicated, may hold values from 0 to 31, as said below
- nb_frame: int32 [32, 8], replicated, may hold values from 0 to 3, as said below
- nb_count: int32 [32], replicated, may hold values from 2 to 8
- block_slot: int32 [32], replicated, may hold values from 0 to 31, as said below
Outputs:
- attn_out: bfloat16 [4096, 1024], P(('region', 'tok'))
Inputs may be any that keep to these rules, and one draw needn't show every extreme that they name: block_slot is a permutation of the block ids; device i of region+tok stores slot i (one block per device). `nb_block`: the entries of one query block name distinct blocks. For the query blocks of device (r, c) of region+tok, entry 0 names one and the same block and frame stored in region group r - 1, entry 1 one and the same stored in group r + 1 (periodic), the other entries blocks stored in group r, on tok indices other than those of entries 0 and 1. For each group r and tok index t, exactly one device of group r reads its entry 0 from tok index t of group r - 1, and exactly one reads its entry 1 from tok index t of group r + 1. All entries of query blocks of devices with tok index c that name blocks stored on one device name one and the same block and frame. `nb_frame`: see nb_block.
All inputs are finite; a program needn't handle non-finite values.
Results may differ from a plain program's by a relative error of at most 0.0035.
The roundings to bfloat16 on the way count: a program that leaves them out, or rounds other values in their place, can miss the bound.
Values may be sent and summed in bfloat16 or wider, within the bound.
No kernel may reach another device: no remote copies, remote signals or barrier semaphores. Data moves between devices by JAX's collectives and lax.ppermute only.
A program may use at most 128 MiB of HBM per device.

v0:
```python
import jax
import jax.numpy as jnp
from jax import lax
from jax.sharding import PartitionSpec as P

HEADS = 8
QB = 128


def shifted(block, axis, distance):
    devices = range(lax.axis_size(axis))
    route = [((i - distance) % len(devices), i) for i in devices]
    return lax.ppermute(block, axis, route)


def per_device(
    tokens,
    w_query,
    w_key,
    w_value,
    w_out,
    past_keys,
    past_values,
    nb_block,
    nb_frame,
    nb_count,
    block_slot,
):
    n_region = lax.axis_size("region")
    n_tok = lax.axis_size("tok")
    region_id = lax.axis_index("region")
    tok_id = lax.axis_index("tok")
    n_devices = n_region * n_tok
    my_device = region_id * n_tok + tok_id
    tok_rows, model_width = tokens.shape
    blocks_dev = tok_rows // QB
    n_blocks, max_entries = nb_block.shape
    head_size = model_width // HEADS
    whole_query, whole_key, whole_value = (
        lax.all_gather(w_query, "tok", axis=0, tiled=True),
        lax.all_gather(w_key, "tok", axis=0, tiled=True),
        lax.all_gather(w_value, "tok", axis=0, tiled=True),
    )
    proj_query = jnp.dot(tokens, whole_query, preferred_element_type=jnp.float32)
    proj_key = jnp.dot(tokens, whole_key, preferred_element_type=jnp.float32)
    proj_value = jnp.dot(tokens, whole_value, preferred_element_type=jnp.float32)
    queries = proj_query.astype(jnp.bfloat16)
    keys_new = proj_key.astype(jnp.bfloat16)
    values_new = proj_value.astype(jnp.bfloat16)
    slot_table = jnp.take(block_slot, nb_block, axis=0)
    source_dev = slot_table // blocks_dev
    source_tok = source_dev % n_tok
    flat_table = nb_frame * blocks_dev + slot_table % blocks_dev
    live_table = jnp.arange(max_entries, dtype=jnp.int32)[None, :] < nb_count[:, None]
    dest_tok = jnp.arange(n_blocks, dtype=jnp.int32) // blocks_dev % n_tok
    tok_range = jnp.arange(n_tok, dtype=jnp.int32)
    mine_flat = (live_table & (source_dev == my_device)).reshape(-1)
    dest_flat = jnp.broadcast_to(dest_tok[:, None], (n_blocks, max_entries)).reshape(-1)
    matches = mine_flat[None, :] & (dest_flat[None, :] == tok_range[:, None])
    offer_index = jnp.max(jnp.where(matches, flat_table.reshape(-1)[None, :], 0), axis=1)
    offer_keys = jnp.take(past_keys, offer_index, axis=0)
    offer_values = jnp.take(past_values, offer_index, axis=0)
    lead_tok = source_tok.reshape(n_devices, blocks_dev, max_entries)[:, 0, :2]
    lower_region = (region_id + n_region - 1) % n_region
    upper_region = (region_id + 1) % n_region
    my_start = my_device * blocks_dev
    my_tok_table = lax.dynamic_slice_in_dim(source_tok, my_start, blocks_dev, 0)
    got_keys, got_values = (
        lax.all_to_all(offer_keys, "tok", split_axis=0, concat_axis=0, tiled=True),
        lax.all_to_all(offer_values, "tok", split_axis=0, concat_axis=0, tiled=True),
    )
    upward_index = lax.dynamic_index_in_dim(
        lead_tok[:, 0], upper_region * n_tok + tok_id, 0, keepdims=False
    )
    downward_index = lax.dynamic_index_in_dim(
        lead_tok[:, 1], lower_region * n_tok + tok_id, 0, keepdims=False
    )
    upward_pair = jnp.concatenate(
        [
            lax.dynamic_slice_in_dim(got_keys, upward_index, 1, 0),
            lax.dynamic_slice_in_dim(got_values, upward_index, 1, 0),
        ],
        0,
    )
    downward_pair = jnp.concatenate(
        [
            lax.dynamic_slice_in_dim(got_keys, downward_index, 1, 0),
            lax.dynamic_slice_in_dim(got_values, downward_index, 1, 0),
        ],
        0,
    )
    below_pair = shifted(upward_pair, "region", 1)
    above_pair = shifted(downward_pair, "region", -1)
    own_index = my_tok_table[:, 2:].reshape(-1)
    own_keys = jnp.take(got_keys, own_index, axis=0).reshape(
        blocks_dev, (max_entries - 2) * QB, model_width
    )
    own_values = jnp.take(got_values, own_index, axis=0).reshape(
        blocks_dev, (max_entries - 2) * QB, model_width
    )
    side_keys = jnp.concatenate([below_pair[0], above_pair[0]], 0)[None]
    side_values = jnp.concatenate([below_pair[1], above_pair[1]], 0)[None]
    far_keys = jnp.concatenate([side_keys, own_keys], 1)
    far_values = jnp.concatenate([side_values, own_values], 1)
    key_list = jnp.concatenate([keys_new.reshape(blocks_dev, QB, model_width), far_keys], 1)
    value_list = jnp.concatenate([values_new.reshape(blocks_dev, QB, model_width), far_values], 1)
    list_len = key_list.shape[1]
    query_heads = queries.reshape(blocks_dev, QB, HEADS, head_size)
    key_heads = key_list.reshape(blocks_dev, list_len, HEADS, head_size)
    value_heads = value_list.reshape(blocks_dev, list_len, HEADS, head_size)
    attn_scale = head_size ** (-0.5)
    scores = (
        jnp.einsum("bqhd,bkhd->bhqk", query_heads, key_heads, preferred_element_type=jnp.float32)
        * attn_scale
    )
    my_counts = lax.dynamic_slice_in_dim(nb_count, my_start, blocks_dev, 0)
    entry_live = jnp.arange(max_entries, dtype=jnp.int32)[None, :] < my_counts[:, None]
    live_mask = jnp.concatenate(
        [jnp.ones((blocks_dev, QB), bool), jnp.repeat(entry_live, QB, axis=1)], 1
    )
    scores = jnp.where(live_mask[:, None, None, :], scores, jnp.float32(-1e30))
    row_max = jnp.max(scores, axis=-1, keepdims=True)
    exp_weights = jnp.where(
        live_mask[:, None, None, :], jnp.exp(scores - row_max), jnp.float32(0.0)
    )
    row_total = jnp.sum(exp_weights, axis=-1)
    prob_bf = exp_weights.astype(jnp.bfloat16)
    context = jnp.einsum(
        "bhqk,bkhd->bqhd", prob_bf, value_heads, preferred_element_type=jnp.float32
    )
    context = context / jnp.swapaxes(row_total, 1, 2)[:, :, :, None]
    context_bf = context.reshape(tok_rows, model_width).astype(jnp.bfloat16)
    whole_out = lax.all_gather(w_out, "tok", axis=1, tiled=True)
    mixed_out = jnp.dot(context_bf, whole_out, preferred_element_type=jnp.float32)
    return mixed_out.astype(jnp.bfloat16)


def solution(mesh):
    return jax.shard_map(
        per_device,
        mesh=mesh,
        in_specs=(
            P(("region", "tok"), None),
            P("tok", None),
            P("tok", None),
            P("tok", None),
            P(None, "tok"),
            P(None, ("region", "tok"), None),
            P(None, ("region", "tok"), None),
            P(),
            P(),
            P(),
            P(),
        ),
        out_specs=P(("region", "tok"), None),
        check_vma=False,
    )
```

profile of v0, /device:TPU:0, one launch (start us, length us, event | category | flops | bytes accessed | tf_op | source)
XLA Modules:
  0.0 164.5 jit_solution(5004245826716925079)
XLA Ops:
  6.5 0.7 all-gather.9.cloned.1.call-update
  7.3 0.7 all-gather.5.cloned.1.call-update
  8.1 0.7 all-gather.7.cloned.1.call-update
  8.8 0.8 copy.48
  9.7 1.9 %gather_fusion = s32[256]{0:T(256)S(1)} fusion(s32[32]{0:T(128)S(1)} %copy-done.1, s32[1024]{0:T(1024)S(1)} %pad_clamp_fusion.2), kind=kCustom, calls=%fused_computation.4 | custom fusion | bytes 3072 | tf_op jit(solution)/shard_map/jit(_take)/gather | solution.py:50
  12.1 0.1 select_reduce_fusion
  12.3 0.7 gather_fusion.1
  13.0 3.3 %gather_fusion.2 = bf16[8,128,1024]{2,1,0:T(8,128)(2,1)} fusion(bf16[4,128,1024]{2,1,0:T(8,128)(2,1)} %param.21, s32[1024]{0:T(1024)S(1)} %pad_clamp_fusion.1), kind=kCustom, calls=%fused_computation.2.clone | custom fusion | bytes 4194336 | tf_op jit(solution)/shard_map/jit(_take)/gather | solution.py:62
  16.3 3.4 %broadcast_select_fusion = (bf16[8,128,1024]{2,1,0:T(8,128)(2,1)S(1)}, bf16[8,128,1024]{2,1,0:T(8,128)(2,1)}) fusion(bf16[8,128,1024]{2,1,0:T(8,128)(2,1)} %gather_fusion.2, pred[8]{0:T(512)(128)(4,1)S(1)} %compare_and_fusion.1, bf16[8,128,1024]{2,1,0:T(8,128)(2,1)S(1)} %gather_fusion.1), kind=kLoop, calls=%fused_computation.26 | loop fusion | flops 2097152 | bytes 8388616 | tf_op jit(solution)/shard_map/jit(_take)/select_n | solution.py:62
  19.7 37.2 %all_to_all.10 = bf16[8,128,1024]{2,1,0:T(8,128)(2,1)S(1)} all-to-all(bf16[8,128,1024]{2,1,0:T(8,128)(2,1)S(1)} %get-tuple-element.21), channel_id=1, replica_groups=mesh['region'=4,'tok'=8] {'tok'}, dimensions={0} | all-to-all | bytes 4194304 | tf_op jit(solution)/shard_map/all_to_all | solution.py:70
  56.9 4.4 %all-to-all-start = ((bf16[8,128,1024]{2,1,0:T(8,128)(2,1)}), bf16[8,128,1024]{2,1,0:T(8,128)(2,1)}, u32[]{:S(2)}, u32[]{:S(2)}) async-start(bf16[8,128,1024]{2,1,0:T(8,128)(2,1)} %get-tuple-element.22), calls=%async_computation | async-start | bytes 4194304 | tf_op jit(solution)/shard_map/all_to_all | solution.py:69
  61.4 0.5 all-gather.11.cloned.1.call-update
  62.1 0.6 constant_dynamic-slice_fusion.3
  65.1 0.6 dynamic_slice.32
  66.9 0.7 iota_compare_fusion.2
  67.6 0.7 constant_dynamic-slice_fusion.4
  68.4 26.7 %all-to-all-done = bf16[8,128,1024]{2,1,0:T(8,128)(2,1)} async-done(((bf16[8,128,1024]{2,1,0:T(8,128)(2,1)}), bf16[8,128,1024]{2,1,0:T(8,128)(2,1)}, u32[]{:S(2)}, u32[]{:S(2)}) %all-to-all-start) | async-done | bytes 2097184 | tf_op jit(solution)/shard_map/all_to_all | solution.py:69
  95.0 1.1 constant_dynamic-slice_fusion.5
  96.1 1.8 %pad_maximum_fusion = bf16[2,128,1024]{2,1,0:T(8,128)(2,1)} fusion(bf16[1,128,1024]{2,1,0:T(8,128)(2,1)} %get-tuple-element.11, bf16[1,128,1024]{2,1,0:T(8,128)(2,1)S(1)} %get-tuple-element.9), kind=kLoop, calls=%fused_computation.39 | loop fusion | flops 262144 | bytes 1048576 | tf_op jit(solution)/shard_map/concatenate | solution.py:78
  97.9 1.5 collective-permute-start
  99.4 0.9 pad_maximum_fusion.1
  100.3 2.3 %collective-permute-start.1 = (bf16[2,128,1024]{2,1,0:T(8,128)(2,1)}, bf16[2,128,1024]{2,1,0:T(8,128)(2,1)}, u32[]{:S(2)}, u32[]{:S(2)}) collective-permute-start(bf16[2,128,1024]{2,1,0:T(8,128)(2,1)} %pad_maximum_fusion.1), channel_id=1, source_target_pairs={{8,0},{16,8},{24,16},{0,24},{9,1},{17,9},{25,17},{1,25},{10,2},{18... | collective-permute-start | bytes 1572872 | tf_op jit(solution)/shard_map/ppermute | solution.py:13
  102.6 3.5 %gather_fusion.4 = bf16[6,128,1024]{2,1,0:T(8,128)(2,1)} fusion(bf16[8,128,1024]{2,1,0:T(8,128)(2,1)} %all-to-all-done, s32[1024]{0:T(1024)S(1)} %pad_clamp_fusion), kind=kCustom, calls=%fused_computation.3.clone | custom fusion | bytes 3145752 | tf_op jit(solution)/shard_map/jit(_take)/gather | solution.py:95
  106.1 1.9 %gather_fusion.3 = bf16[6,128,1024]{2,1,0:T(8,128)(2,1)} fusion(bf16[8,128,1024]{2,1,0:T(8,128)(2,1)S(1)} %all_to_all.10, s32[1024]{0:T(1024)S(1)} %pad_clamp_fusion), kind=kCustom, calls=%fused_computation.1.clone | custom fusion | bytes 3145752 | tf_op jit(solution)/shard_map/jit(_take)/gather | solution.py:98
  107.9 2.2 %broadcast_select_fusion.3 = (bf16[6,128,1024]{2,1,0:T(8,128)(2,1)S(1)}, bf16[6,128,1024]{2,1,0:T(8,128)(2,1)S(1)}) fusion(bf16[6,128,1024]{2,1,0:T(8,128)(2,1)} %gather_fusion.3, pred[6]{0:T(512)(128)(4,1)S(1)} %get-tuple-element.6, bf16[6,128,1024]{2,1,0:T(8,128)(2,1)} %gather_fusion.4), kind=kLoop, calls=%fused_computation.29 | loop fusion | flops 1572864 | bytes 6291462 | tf_op jit(solution)/shard_map/jit(_take)/select_n | solution.py:98
  110.2 0.4 copy.69
  110.6 1.4 copy.62
  112.0 0.4 copy.66
  112.5 1.9 %copy.56 = bf16[1,768,8,128]{1,3,2,0:T(8,128)(2,1)} copy(bf16[1,768,8,128]{3,2,1,0:T(8,128)(2,1)S(1)} %bitcast.77) | data formatting | bytes 3145728 | tf_op jit(solution)/shard_map/concatenate | solution.py:106
  114.3 0.4 collective-permute-done
  114.8 1.1 fusion.35
  115.9 0.2 copy.57
  116.0 0.2 copy.60
  116.2 5.8 %collective-permute-done.1 = bf16[2,128,1024]{2,1,0:T(8,128)(2,1)} collective-permute-done((bf16[2,128,1024]{2,1,0:T(8,128)(2,1)}, bf16[2,128,1024]{2,1,0:T(8,128)(2,1)}, u32[]{:S(2)}, u32[]{:S(2)}) %collective-permute-start.1) | collective-permute-done | bytes 524320 | tf_op jit(solution)/shard_map/ppermute | solution.py:13
  122.0 1.1 fusion.36
  123.1 0.2 copy.58
  123.3 0.9 copy.61
  124.1 0.2 copy.53
  124.3 0.8 copy.54
  125.2 2.0 %fusion.21 = bf16[16,8,8,128]{3,1,2,0:T(8,128)(2,1)S(1)} fusion(bf16[128,1024]{1,0:T(8,128)(2,1)S(1)} %copy-done.2, bf16[1024,1024]{1,0:T(8,128)(2,1)} %all-gather.9.cloned.1.call-done), kind=kOutput, calls=%fused_computation.36 | convolution fusion | flops 268566528 | bytes 2621440 | tf_op jit(solution)/shard_map/dot_general | solution.py:45
  127.3 0.8 copy.59
  128.0 2.0 %convolution_convert_fusion.3 = bf16[128,1024]{1,0:T(8,128)(2,1)S(1)} fusion(bf16[128,1024]{1,0:T(8,128)(2,1)S(1)} %copy-done.2, bf16[1024,1024]{1,0:T(8,128)(2,1)} %all-gather.5.cloned.1.call-done), kind=kOutput, calls=%fused_computation.34 | convolution fusion | flops 268566528 | bytes 2621440 | tf_op jit(solution)/shard_map/dot_general | solution.py:46
  130.1 0.9 copy.64
  130.9 2.0 %fusion.20 = bf16[16,8,8,128]{3,2,1,0:T(8,128)(2,1)S(1)} fusion(bf16[128,1024]{1,0:T(8,128)(2,1)S(1)} %copy-done.2, bf16[1024,1024]{1,0:T(8,128)(2,1)} %all-gather.7.cloned.1.call-done), kind=kOutput, calls=%fused_computation.35 | convolution fusion | flops 268566528 | bytes 2621440 | tf_op jit(solution)/shard_map/dot_general | solution.py:44
  133.0 5.0 %fusion.38 = (f32[8,128]{1,0:T(8,128)S(1)}, bf16[8,128,1152]{2,1,0:T(8,128)(2,1)}) fusion(pred[1152]{0:T(1024)(128)(4,1)S(1)} %pad_reduce_fusion, bf16[1,768,8,128]{3,1,2,0:T(8,128)(2,1)} %copy.62, bf16[1,128,8,128]{3,1,2,0:T(8,128)(2,1)} %copy.61, bf16[1,128,8,128]{3,1,2,0:T(8,128)(2,1)S(1)} %copy.60, bf16[1,128,8,128]{3,1,2,0:T(8,128)(2,1)} %copy.59, ...), kind=kOutput, calls=%fused_computation.78 | convolution fusion | flops 318506112 | bytes 4985984 | tf_op jit(solution)/shard_map/sub | solution.py:124
  137.9 2.8 %fusion.25 = bf16[1,128,8,128]{1,3,2,0:T(8,128)(2,1)S(1)} fusion(bf16[8,128,1152]{2,1,0:T(8,128)(2,1)} %get-tuple-element.24, bf16[1,768,8,128]{1,3,2,0:T(8,128)(2,1)S(1)} %copy-done.3, bf16[1,128,8,128]{1,3,2,0:T(8,128)(2,1)} %bitcast.85, bf16[1,128,8,128]{1,3,2,0:T(8,128)(2,1)S(1)} %bitcast.84, bf16[1,128,8,128]{1,3,2,0:T(8,128)(2,1)} %bitcast.86, ...), kind=kOutput, calls=%fused_computation.38 | convolution fusion | flops 311689216 | bytes 4984832 | tf_op jit(solution)/shard_map/bhqk,bkhd->bqhd/dot_general | solution.py:128
  140.7 14.5 %all-gather.11.cloned.1.call-done = bf16[1024,1024]{1,0:T(8,128)(2,1)} async-done(((bf16[1024,128]{1,0:T(8,128)(2,1)}), bf16[1024,1024]{1,0:T(8,128)(2,1)}) %all-gather.11.cloned.1.call-update) | async-done | bytes 2097168 | tf_op jit(solution)/shard_map/all_gather | solution.py:133
  155.2 2.8 %convolution_convert_fusion = bf16[128,1024]{1,0:T(8,128)(2,1)} fusion(bf16[128,1024]{0,1:T(8,128)(2,1)S(1)} %bitcast.83, bf16[1024,1024]{1,0:T(8,128)(2,1)} %all-gather.11.cloned.1.call-done), kind=kOutput, calls=%fused_computation.31 | convolution fusion | flops 268566528 | bytes 2621440 | tf_op jit(solution)/shard_map/dot_general | solution.py:134
  (43 shorter events, 1.2 us)
Async XLA Ops:
  6.5 5.8 %copy-start = (bf16[4,128,1024]{2,1,0:T(8,128)(2,1)S(1)}, bf16[4,128,1024]{2,1,0:T(8,128)(2,1)}, u32[]{:S(2)}) copy-start(bf16[4,128,1024]{2,1,0:T(8,128)(2,1)} %param.20) | copy-start | bytes 3145732
  6.5 3.1 %copy-start.1 = (s32[32]{0:T(128)S(1)}, s32[32]{0:T(128)}, u32[]{:S(2)}) copy-start(s32[32]{0:T(128)} %param.25) | copy-start | bytes 388
  6.5 118.6 %all-gather.9.cloned.1.call-start = ((), (), s32[]{:S(2)}) async-start(), calls=%async_computation.4 | async-start | bytes 2359296 | tf_op jit(solution)/shard_map/all_gather | solution.py:41
  7.3 120.7 %all-gather.5.cloned.1.call-start = ((), (), s32[]{:S(2)}) async-start(), calls=%async_computation.2 | async-start | bytes 2359296 | tf_op jit(solution)/shard_map/all_gather | solution.py:42
  8.0 122.9 %all-gather.7.cloned.1.call-start = ((), (), s32[]{:S(2)}) async-start(), calls=%async_computation.3 | async-start | bytes 2359296 | tf_op jit(solution)/shard_map/all_gather | solution.py:40
  9.6 2.0 %copy-start.5 = (s32[32]{0:T(128)S(1)}, s32[32]{0:T(128)}, u32[]{:S(2)}) copy-start(s32[32]{0:T(128)} %param.24) | copy-start | bytes 388
  9.6 2.3 %copy-start.4 = (s32[32,8]{0,1:T(8,128)S(1)}, s32[32,8]{0,1:T(8,128)}, u32[]{:S(2)}) copy-start(s32[32,8]{0,1:T(8,128)} %param.23) | copy-start | bytes 3076
  56.9 38.1 %all-to-all-start = ((bf16[8,128,1024]{2,1,0:T(8,128)(2,1)}), bf16[8,128,1024]{2,1,0:T(8,128)(2,1)}, u32[]{:S(2)}, u32[]{:S(2)}) async-start(bf16[8,128,1024]{2,1,0:T(8,128)(2,1)} %get-tuple-element.22), calls=%async_computation | async-start | bytes 4194304 | tf_op jit(solution)/shard_map/all_to_all | solution.py:69
  61.3 93.9 %all-gather.11.cloned.1.call-start = ((), (), s32[]{:S(2)}) async-start(), calls=%async_computation.5 | async-start | bytes 2359296 | tf_op jit(solution)/shard_map/all_gather | solution.py:133
  97.9 16.9 %collective-permute-start = (bf16[2,128,1024]{2,1,0:T(8,128)(2,1)}, bf16[2,128,1024]{2,1,0:T(8,128)(2,1)}, u32[]{:S(2)}, u32[]{:S(2)}) collective-permute-start(bf16[2,128,1024]{2,1,0:T(8,128)(2,1)} %pad_maximum_fusion), channel_id=1, source_target_pairs={{24,0},{0,8},{8,16},{16,24},{25,1},{1,9},{9,17},{17,25},{26,2},{2,... | collective-permute-start | bytes 1572872 | tf_op jit(solution)/shard_map/ppermute | solution.py:13
  100.3 21.8 %collective-permute-start.1 = (bf16[2,128,1024]{2,1,0:T(8,128)(2,1)}, bf16[2,128,1024]{2,1,0:T(8,128)(2,1)}, u32[]{:S(2)}, u32[]{:S(2)}) collective-permute-start(bf16[2,128,1024]{2,1,0:T(8,128)(2,1)} %pad_maximum_fusion.1), channel_id=1, source_target_pairs={{8,0},{16,8},{24,16},{0,24},{9,1},{17,9},{25,17},{1,25},{10,2},{18... | collective-permute-start | bytes 1572872 | tf_op jit(solution)/shard_map/ppermute | solution.py:13
  115.8 9.3 %copy-start.2 = (bf16[128,1024]{1,0:T(8,128)(2,1)S(1)}, bf16[128,1024]{1,0:T(8,128)(2,1)}, u32[]{:S(2)}) copy-start(bf16[128,1024]{1,0:T(8,128)(2,1)} %param.15) | copy-start | bytes 786436
  133.0 5.0 %copy-start.3 = (bf16[1,768,8,128]{1,3,2,0:T(8,128)(2,1)S(1)}, bf16[1,768,8,128]{1,3,2,0:T(8,128)(2,1)}, u32[]{:S(2)}) copy-start(bf16[1,768,8,128]{1,3,2,0:T(8,128)(2,1)} %copy.56) | copy-start | bytes 4718596
Sparse Core Ops, SparseCore 0:
  9.2 41.8 all-gather.8
  53.0 40.6 all-gather.4
  95.6 29.6 all-gather.6
  127.0 28.0 all-gather.10
where the time goes:
time: 165 us; the launch traced here: 164 us
  waiting for transfers between devices  50 us (30%)
  blocking collectives  37.2 us (23%)
  local copies, waits for them, and re-layouts  26.1 us (16%)
  between operations  17 us (10%)
  matrix products  16.6 us (10%)
  other arithmetic  9.24 us (6%)
  starting transfers between devices  8.33 us (5%)
    all_to_all x1, blocking collectives, per_device(): lax.all_to_all(offer_values, 'tok', split_axis=0, concat_axis=0, tiled=True)  37.2 us
    all_to_all x1, waiting for transfers between devices, per_device(): lax.all_to_all(offer_keys, 'tok', split_axis=0, concat_axis=0, tiled=True)  26.7 us
    all_gather x1, waiting for transfers between devices, per_device(): whole_out = lax.all_gather(w_out, 'tok', axis=1, tiled=True)  14.5 us
    ppermute x2, waiting for transfers between devices, shifted(): return lax.ppermute(block, axis, route)  6.26 us
    sub x1, matrix products, per_device(): scores - row_max  4.96 us
    all_to_all x1, starting transfers between devices, per_device(): lax.all_to_all(offer_keys, 'tok', split_axis=0, concat_axis=0, tiled=True)  4.38 us
    ppermute x2, starting transfers between devices, shifted(): return lax.ppermute(block, axis, route)  3.82 us
    gather x1, local copies, waits for them, and re-layouts, per_device(): jnp.take(got_keys, own_index, axis=0)  3.47 us
  transfers between devices with their start and end apart: 7, of which 4 were waited for; matrix products, arithmetic and copies ran while one was open for 30% of the time, Pallas kernels for 0%

commit v1 on v0

--- a/solution.py
+++ b/solution.py
@@ -5,6 +5,28 @@
 
 HEADS = 8
 QB = 128
+
+
+def split_up(shard, dim, devices):
+    before, after = (shard.shape[:dim], shard.shape[dim + 1 :])
+    return jnp.moveaxis(shard.reshape(*before, devices, -1, *after), dim, 0)
+
+
+def in_order(parts, dim):
+    lengths = list(parts.shape[1:])
+    lengths[dim] *= parts.shape[0]
+    return jnp.moveaxis(parts, 0, dim).reshape(lengths)
+
+
+def exchange_directly(x, axis, split_dim, concat_dim):
+    count, here = (lax.axis_size(axis), lax.axis_index(axis))
+    pieces = split_up(x, split_dim, count)
+    done = [pieces[here]]
+    for step in range(1, count):
+        sent = pieces[(here + step) % count]
+        done.append(lax.ppermute(sent, axis, [(i, (i + step) % count) for i in range(count)]))
+    pieces = jnp.stack(done)[(here - jnp.arange(count)) % count]
+    return in_order(pieces, concat_dim)
 
 
 def shifted(block, axis, distance):
@@ -67,7 +89,7 @@
     my_tok_table = lax.dynamic_slice_in_dim(source_tok, my_start, blocks_dev, 0)
     got_keys, got_values = (
         lax.all_to_all(offer_keys, "tok", split_axis=0, concat_axis=0, tiled=True),
-        lax.all_to_all(offer_values, "tok", split_axis=0, concat_axis=0, tiled=True),
+        exchange_directly(offer_values, "tok", 0, 0),
     )
     upward_index = lax.dynamic_index_in_dim(
         lead_tok[:, 0], upper_region * n_tok + tok_id, 0, keepdims=False

time: 165 us -> 160 us (0.970)
  blocking collectives: 37.2 us -> 0 us
  local copies, waits for them, and re-layouts: 26.1 us -> 43.5 us
  starting transfers between devices: 8.33 us -> 17.4 us
  waiting for transfers between devices: 50 us -> 54 us
    all_to_all x1 -> x0, blocking collectives: 37.2 us -> none  [per_device(): lax.all_to_all(offer_values, 'tok', split_axis=0, concat_axis=0, tiled=True)]
    ppermute x0 -> x7, waiting for transfers between devices: none -> 29.1 us  [exchange_directly(): lax.ppermute(sent, axis, [(i, (i + step) % count) for i in range(count)])]
    all_to_all x1, waiting for transfers between devices: 26.7 us -> 0.01 us  [per_device(): lax.all_to_all(offer_keys, 'tok', split_axis=0, concat_axis=0, tiled=True)]
    unnamed x19 -> x28, local copies, waits for them, and re-layouts: 1.87 us -> 13 us
    ppermute x0 -> x7, starting transfers between devices: none -> 9.53 us  [exchange_directly(): lax.ppermute(sent, axis, [(i, (i + step) % count) for i in range(count)])]
    gather x0 -> x1, local copies, waits for them, and re-layouts: none -> 3.65 us  [exchange_directly(): pieces = jnp.stack(done)[(here - jnp.arange(count)) % count]]
    ppermute x2, waiting for transfers between devices: 6.26 us -> 9.26 us  [shifted(): return lax.ppermute(block, axis, route)]
  transfers between devices with their start and end apart: 7 -> 14, of which waited for: 4 -> 6; matrix products, arithmetic and copies ran while one was open for 30% -> 42% of each run, Pallas kernels for 0% -> 0%
where the time goes in v1:
time: 160 us; the launch traced here: 159 us
  waiting for transfers between devices  54 us (34%)
  local copies, waits for them, and re-layouts  43.5 us (27%)
  starting transfers between devices  17.4 us (11%)
  between operations  17.2 us (11%)
  matrix products  16.6 us (10%)
  other arithmetic  10.2 us (6%)
    ppermute x7, waiting for transfers between devices, exchange_directly(): lax.ppermute(sent, axis, [(i, (i + step) % count) for i in range(count)])  29.1 us
    all_gather x1, waiting for transfers between devices, per_device(): whole_out = lax.all_gather(w_out, 'tok', axis=1, tiled=True)  13 us
    unnamed x28, local copies, waits for them, and re-layouts  13 us
    ppermute x7, starting transfers between devices, exchange_directly(): lax.ppermute(sent, axis, [(i, (i + step) % count) for i in range(count)])  9.53 us
    ppermute x2, waiting for transfers between devices, shifted(): return lax.ppermute(block, axis, route)  9.26 us
    sub x1, matrix products, per_device(): scores - row_max  4.94 us
    all_to_all x1, starting transfers between devices, per_device(): lax.all_to_all(offer_keys, 'tok', split_axis=0, concat_axis=0, tiled=True)  3.92 us
    ppermute x2, starting transfers between devices, shifted(): return lax.ppermute(block, axis, route)  3.82 us
  transfers between devices with their start and end apart: 14, of which 6 were waited for; matrix products, arithmetic and copies ran while one was open for 42% of the time, Pallas kernels for 0%

profile of v1, /device:TPU:0, one launch (start us, length us, event | category | flops | bytes accessed | tf_op | source)
XLA Modules:
  0.0 158.8 jit_solution(5213950817103844096)
XLA Ops:
  8.8 0.8 copy.54
  9.7 1.9 %gather_fusion = s32[256]{0:T(256)S(1)} fusion(s32[32]{0:T(128)S(1)} %copy-done.1, s32[1024]{0:T(1024)S(1)} %pad_clamp_fusion.3), kind=kCustom, calls=%fused_computation.4 | custom fusion | bytes 3072 | tf_op jit(solution)/shard_map/jit(_take)/gather | solution.py:72
  13.1 3.2 %gather_fusion.3 = bf16[8,128,1024]{2,1,0:T(8,128)(2,1)} fusion(bf16[4,128,1024]{2,1,0:T(8,128)(2,1)} %param.21, s32[1024]{0:T(1024)S(1)} %pad_clamp_fusion.2), kind=kCustom, calls=%fused_computation.2.clone | custom fusion | bytes 4194336 | tf_op jit(solution)/shard_map/jit(_take)/gather | solution.py:84
  16.3 3.3 %broadcast_select_fusion = (bf16[8,128,1024]{2,1,0:T(8,128)(2,1)S(1)}, bf16[8,128,1024]{2,1,0:T(8,128)(2,1)}) fusion(bf16[8,128,1024]{2,1,0:T(8,128)(2,1)} %gather_fusion.3, pred[8]{0:T(512)(128)(4,1)S(1)} %compare_and_fusion.1, bf16[8,128,1024]{2,1,0:T(8,128)(2,1)S(1)} %gather_fusion.2), kind=kLoop, calls=%fused_computation.27 | loop fusion | flops 2097152 | bytes 8388616 | tf_op jit(solution)/shard_map/jit(_take)/select_n | solution.py:84
  19.6 1.4 copy-done.2
  21.0 1.2 constant_dynamic-slice_fusion.5
  22.7 2.6 %collective-permute-start.1 = (bf16[1,128,1024]{2,1,0:T(8,128)(2,1)}, bf16[1,128,1024]{2,1,0:T(8,128)(2,1)}, u32[]{:S(2)}, u32[]{:S(2)}) collective-permute-start(bf16[1,128,1024]{2,1,0:T(8,128)(2,1)} %get-tuple-element.18), channel_id=1, source_target_pairs={{0,2},{1,3},{2,4},{3,5},{4,6},{5,7},{6,0},{7,1},{8,10},{9,11},{10,... | collective-permute-start | bytes 786440 | tf_op jit(solution)/shard_map/ppermute | solution.py:27
  25.3 2.4 %collective-permute-start.2 = (bf16[1,128,1024]{2,1,0:T(8,128)(2,1)}, bf16[1,128,1024]{2,1,0:T(8,128)(2,1)}, u32[]{:S(2)}, u32[]{:S(2)}) collective-permute-start(bf16[1,128,1024]{2,1,0:T(8,128)(2,1)} %get-tuple-element.17), channel_id=1, source_target_pairs={{0,3},{1,4},{2,5},{3,6},{4,7},{5,0},{6,1},{7,2},{8,11},{9,12},{10,... | collective-permute-start | bytes 786440 | tf_op jit(solution)/shard_map/ppermute | solution.py:27
  28.3 3.9 %all-to-all-start = ((bf16[8,128,1024]{2,1,0:T(8,128)(2,1)}), bf16[8,128,1024]{2,1,0:T(8,128)(2,1)S(1)}, u32[]{:S(2)}, u32[]{:S(2)}) async-start(bf16[8,128,1024]{2,1,0:T(8,128)(2,1)} %get-tuple-element.29), calls=%async_computation | async-start | bytes 4194304 | tf_op jit(solution)/shard_map/all_to_all | solution.py:91
  34.3 1.7 %bitcast_dynamic-update-slice_fusion.7 = bf16[8,1,128,1024]{3,2,0,1:T(8,128)(2,1)} fusion(bf16[8,128,1024]{2,1,0:T(8,128)(2,1)} %copy-done.2, s32[]{:T(128)S(6)} %select_n.187), kind=kLoop, calls=%fused_computation.51 | loop fusion | bytes 524292
  40.4 3.0 %collective-permute-start.5 = (bf16[1,128,1024]{2,1,0:T(8,128)(2,1)}, bf16[1,128,1024]{2,1,0:T(8,128)(2,1)S(1)}, u32[]{:S(2)}, u32[]{:S(2)}) collective-permute-start(bf16[1,128,1024]{2,1,0:T(8,128)(2,1)} %get-tuple-element.14), channel_id=1, source_target_pairs={{0,6},{1,7},{2,0},{3,1},{4,2},{5,3},{6,4},{7,5},{8,14},{9,15},{10,... | collective-permute-start | bytes 786440 | tf_op jit(solution)/shard_map/ppermute | solution.py:27
  43.3 1.7 %bitcast_dynamic-update-slice_fusion.5 = bf16[8,1,128,1024]{3,2,0,1:T(8,128)(2,1)} fusion(bf16[8,1,128,1024]{3,2,0,1:T(8,128)(2,1)} %bitcast_dynamic-update-slice_fusion.7, bf16[1,128,1024]{2,1,0:T(8,128)(2,1)} %collective-permute-done), kind=kLoop, calls=%fused_computation.49 | loop fusion | bytes 524288
  45.5 1.7 %bitcast_dynamic-update-slice_fusion.4 = bf16[8,1,128,1024]{3,2,0,1:T(8,128)(2,1)} fusion(bf16[8,1,128,1024]{3,2,0,1:T(8,128)(2,1)} %bitcast_dynamic-update-slice_fusion.5, bf16[1,128,1024]{2,1,0:T(8,128)(2,1)} %collective-permute-done.1), kind=kLoop, calls=%fused_computation.48 | loop fusion | bytes 524288
  47.2 2.2 %collective-permute-done.2 = bf16[1,128,1024]{2,1,0:T(8,128)(2,1)} collective-permute-done((bf16[1,128,1024]{2,1,0:T(8,128)(2,1)}, bf16[1,128,1024]{2,1,0:T(8,128)(2,1)}, u32[]{:S(2)}, u32[]{:S(2)}) %collective-permute-start.2) | collective-permute-done | bytes 262176 | tf_op jit(solution)/shard_map/ppermute | solution.py:27
  49.4 1.7 %bitcast_dynamic-update-slice_fusion.3 = bf16[8,1,128,1024]{3,2,0,1:T(8,128)(2,1)} fusion(bf16[8,1,128,1024]{3,2,0,1:T(8,128)(2,1)} %bitcast_dynamic-update-slice_fusion.4, bf16[1,128,1024]{2,1,0:T(8,128)(2,1)} %collective-permute-done.2), kind=kLoop, calls=%fused_computation.47 | loop fusion | bytes 524288
  51.0 1.7 %bitcast_dynamic-update-slice_fusion.2 = bf16[8,1,128,1024]{3,2,0,1:T(8,128)(2,1)} fusion(bf16[8,1,128,1024]{3,2,0,1:T(8,128)(2,1)} %bitcast_dynamic-update-slice_fusion.3, bf16[1,128,1024]{2,1,0:T(8,128)(2,1)} %collective-permute-done.3), kind=kLoop, calls=%fused_computation.46 | loop fusion | bytes 524288
  52.7 8.1 %collective-permute-done.4 = bf16[1,128,1024]{2,1,0:T(8,128)(2,1)S(1)} collective-permute-done((bf16[1,128,1024]{2,1,0:T(8,128)(2,1)}, bf16[1,128,1024]{2,1,0:T(8,128)(2,1)S(1)}, u32[]{:S(2)}, u32[]{:S(2)}) %collective-permute-start.4) | collective-permute-done | bytes 262176 | tf_op jit(solution)/shard_map/ppermute | solution.py:27
  60.8 0.7 bitcast_dynamic-update-slice_fusion.1
  61.5 14.9 %collective-permute-done.5 = bf16[1,128,1024]{2,1,0:T(8,128)(2,1)S(1)} collective-permute-done((bf16[1,128,1024]{2,1,0:T(8,128)(2,1)}, bf16[1,128,1024]{2,1,0:T(8,128)(2,1)S(1)}, u32[]{:S(2)}, u32[]{:S(2)}) %collective-permute-start.5) | collective-permute-done | bytes 262176 | tf_op jit(solution)/shard_map/ppermute | solution.py:27
  76.3 0.7 bitcast_dynamic-update-slice_fusion
  77.1 4.0 %collective-permute-done.6 = bf16[1,128,1024]{2,1,0:T(8,128)(2,1)S(1)} collective-permute-done((bf16[1,128,1024]{2,1,0:T(8,128)(2,1)}, bf16[1,128,1024]{2,1,0:T(8,128)(2,1)S(1)}, u32[]{:S(2)}, u32[]{:S(2)}) %collective-permute-start.6) | collective-permute-done | bytes 262176 | tf_op jit(solution)/shard_map/ppermute | solution.py:27
  81.1 0.7 bitcast_dynamic-update-slice_fusion.6
  81.8 3.7 %gather_fusion.1 = bf16[8,128,1024]{2,1,0:T(8,128)(2,1)} fusion(bf16[8,128,1024]{2,1,0:T(8,128)(2,1)} %bitcast.111, s32[1024]{0:T(1024)S(1)} %pad_clamp_fusion.1), kind=kCustom, calls=%fused_computation.5 | custom fusion | bytes 4194336 | tf_op jit(solution)/shard_map/gather | solution.py:28
  85.4 1.8 %constant_dynamic-slice_fusion.4 = (bf16[1,128,1024]{2,1,0:T(8,128)(2,1)}, bf16[1,128,1024]{2,1,0:T(8,128)(2,1)S(1)}) fusion(bf16[8,128,1024]{2,1,0:T(8,128)(2,1)} %gather_fusion.1, s32[]{:T(128)S(6)} %select_n.186, s32[]{:T(128)S(6)} %select_n.206), kind=kLoop, calls=%fused_computation.73 | loop fusion | bytes 1048584 | tf_op jit(solution)/shard_map/dynamic_slice | solution.py:103
  87.2 0.7 constant_dynamic-slice_fusion.12
  87.9 1.8 %pad_maximum_fusion = bf16[2,128,1024]{2,1,0:T(8,128)(2,1)} fusion(bf16[1,128,1024]{2,1,0:T(8,128)(2,1)} %get-tuple-element.11, bf16[1,128,1024]{2,1,0:T(8,128)(2,1)S(1)} %get-tuple-element.9), kind=kLoop, calls=%fused_computation.40 | loop fusion | flops 262144 | bytes 1048576 | tf_op jit(solution)/shard_map/concatenate | solution.py:100
  89.8 1.4 collective-permute-start.7
  91.2 3.4 %gather_fusion.4 = bf16[6,128,1024]{2,1,0:T(8,128)(2,1)} fusion(bf16[8,128,1024]{2,1,0:T(8,128)(2,1)} %gather_fusion.1, s32[1024]{0:T(1024)S(1)} %pad_clamp_fusion), kind=kCustom, calls=%fused_computation.1.clone | custom fusion | bytes 3145752 | tf_op jit(solution)/shard_map/jit(_take)/gather | solution.py:120
  94.6 1.8 %pad_maximum_fusion.1 = bf16[2,128,1024]{2,1,0:T(8,128)(2,1)} fusion(bf16[1,128,1024]{2,1,0:T(8,128)(2,1)S(1)} %get-tuple-element.12, bf16[1,128,1024]{2,1,0:T(8,128)(2,1)} %get-tuple-element.10), kind=kLoop, calls=%fused_computation.41 | loop fusion | flops 262144 | bytes 1048576 | tf_op jit(solution)/shard_map/concatenate | solution.py:107
  96.4 2.4 %collective-permute-start.8 = (bf16[2,128,1024]{2,1,0:T(8,128)(2,1)}, bf16[2,128,1024]{2,1,0:T(8,128)(2,1)}, u32[]{:S(2)}, u32[]{:S(2)}) collective-permute-start(bf16[2,128,1024]{2,1,0:T(8,128)(2,1)} %pad_maximum_fusion.1), channel_id=1, source_target_pairs={{8,0},{16,8},{24,16},{0,24},{9,1},{17,9},{25,17},{1,25},{10,2},{18... | collective-permute-start | bytes 1572872 | tf_op jit(solution)/shard_map/ppermute | solution.py:35
  98.9 1.9 %gather_fusion.5 = bf16[6,128,1024]{2,1,0:T(8,128)(2,1)} fusion(bf16[8,128,1024]{2,1,0:T(8,128)(2,1)S(1)} %all-to-all-done, s32[1024]{0:T(1024)S(1)} %pad_clamp_fusion), kind=kCustom, calls=%fused_computation.3.clone | custom fusion | bytes 3145752 | tf_op jit(solution)/shard_map/jit(_take)/gather | solution.py:117
  100.8 2.2 %broadcast_select_fusion.3 = (bf16[6,128,1024]{2,1,0:T(8,128)(2,1)S(1)}, bf16[6,128,1024]{2,1,0:T(8,128)(2,1)S(1)}) fusion(bf16[6,128,1024]{2,1,0:T(8,128)(2,1)} %gather_fusion.4, pred[6]{0:T(512)(128)(4,1)S(1)} %get-tuple-element.6, bf16[6,128,1024]{2,1,0:T(8,128)(2,1)} %gather_fusion.5), kind=kLoop, calls=%fused_computation.30 | loop fusion | flops 1572864 | bytes 6291462 | tf_op jit(solution)/shard_map/jit(_take)/select_n | solution.py:120
  103.4 1.4 copy.74
  105.3 1.9 %copy.68 = bf16[1,768,8,128]{1,3,2,0:T(8,128)(2,1)} copy(bf16[1,768,8,128]{3,2,1,0:T(8,128)(2,1)S(1)} %bitcast.108) | data formatting | bytes 3145728 | tf_op jit(solution)/shard_map/concatenate | solution.py:128
  107.1 1.1 fusion.37
  108.6 9.3 %collective-permute-done.8 = bf16[2,128,1024]{2,1,0:T(8,128)(2,1)} collective-permute-done((bf16[2,128,1024]{2,1,0:T(8,128)(2,1)}, bf16[2,128,1024]{2,1,0:T(8,128)(2,1)}, u32[]{:S(2)}, u32[]{:S(2)}) %collective-permute-start.8) | collective-permute-done | bytes 524320 | tf_op jit(solution)/shard_map/ppermute | solution.py:35
  117.8 1.1 fusion.38
  119.1 0.9 copy.73
  120.1 0.9 copy.66
  121.0 2.0 %fusion.21 = bf16[16,8,8,128]{3,1,2,0:T(8,128)(2,1)S(1)} fusion(bf16[128,1024]{1,0:T(8,128)(2,1)S(1)} %copy-done.3, bf16[1024,1024]{1,0:T(8,128)(2,1)} %all-gather.9.cloned.1.call-done), kind=kOutput, calls=%fused_computation.37 | convolution fusion | flops 268566528 | bytes 2621440 | tf_op jit(solution)/shard_map/dot_general | solution.py:67
  123.1 0.7 copy.71
  123.8 2.0 %convolution_convert_fusion.3 = bf16[128,1024]{1,0:T(8,128)(2,1)S(1)} fusion(bf16[128,1024]{1,0:T(8,128)(2,1)S(1)} %copy-done.3, bf16[1024,1024]{1,0:T(8,128)(2,1)} %all-gather.5.cloned.1.call-done), kind=kOutput, calls=%fused_computation.35 | convolution fusion | flops 268566528 | bytes 2621440 | tf_op jit(solution)/shard_map/dot_general | solution.py:68
  125.9 0.8 copy.76
  126.7 2.1 %fusion.20 = bf16[16,8,8,128]{3,2,1,0:T(8,128)(2,1)S(1)} fusion(bf16[128,1024]{1,0:T(8,128)(2,1)S(1)} %copy-done.3, bf16[1024,1024]{1,0:T(8,128)(2,1)} %all-gather.7.cloned.1.call-done), kind=kOutput, calls=%fused_computation.36 | convolution fusion | flops 268566528 | bytes 2621440 | tf_op jit(solution)/shard_map/dot_general | solution.py:66
  128.8 4.9 %fusion.40 = (f32[8,128]{1,0:T(8,128)S(1)}, bf16[8,128,1152]{2,1,0:T(8,128)(2,1)}) fusion(pred[1152]{0:T(1024)(128)(4,1)S(1)} %pad_reduce_fusion, bf16[1,768,8,128]{3,1,2,0:T(8,128)(2,1)} %copy.74, bf16[1,128,8,128]{3,1,2,0:T(8,128)(2,1)} %copy.73, bf16[1,128,8,128]{3,1,2,0:T(8,128)(2,1)S(1)} %copy.72, bf16[1,128,8,128]{3,1,2,0:T(8,128)(2,1)} %copy.71, ...), kind=kOutput, calls=%fused_computation.101 | convolution fusion | flops 318506112 | bytes 4985984 | tf_op jit(solution)/shard_map/sub | solution.py:146
  133.8 2.7 %fusion.25 = bf16[1,128,8,128]{1,3,2,0:T(8,128)(2,1)S(1)} fusion(bf16[8,128,1152]{2,1,0:T(8,128)(2,1)} %get-tuple-element.31, bf16[1,768,8,128]{1,3,2,0:T(8,128)(2,1)S(1)} %copy-done.4, bf16[1,128,8,128]{1,3,2,0:T(8,128)(2,1)} %bitcast.117, bf16[1,128,8,128]{1,3,2,0:T(8,128)(2,1)S(1)} %bitcast.116, bf16[1,128,8,128]{1,3,2,0:T(8,128)(2,1)} %bitcast.118, ...), kind=kOutput, calls=%fused_computation.39 | convolution fusion | flops 311689216 | bytes 4984832 | tf_op jit(solution)/shard_map/bhqk,bkhd->bqhd/dot_general | solution.py:150
  136.5 13.0 %all-gather.11.cloned.1.call-done = bf16[1024,1024]{1,0:T(8,128)(2,1)} async-done(((bf16[1024,128]{1,0:T(8,128)(2,1)}), bf16[1024,1024]{1,0:T(8,128)(2,1)}) %all-gather.11.cloned.1.call-update) | async-done | bytes 2097168 | tf_op jit(solution)/shard_map/all_gather | solution.py:155
  149.5 2.8 %convolution_convert_fusion = bf16[128,1024]{1,0:T(8,128)(2,1)} fusion(bf16[128,1024]{0,1:T(8,128)(2,1)S(1)} %bitcast.115, bf16[1024,1024]{1,0:T(8,128)(2,1)} %all-gather.11.cloned.1.call-done), kind=kOutput, calls=%fused_computation.32 | convolution fusion | flops 268566528 | bytes 2621440 | tf_op jit(solution)/shard_map/dot_general | solution.py:156
  (70 shorter events, 9.7 us)
Async XLA Ops:
  6.5 5.8 %copy-start = (bf16[4,128,1024]{2,1,0:T(8,128)(2,1)S(1)}, bf16[4,128,1024]{2,1,0:T(8,128)(2,1)}, u32[]{:S(2)}) copy-start(bf16[4,128,1024]{2,1,0:T(8,128)(2,1)} %param.20) | copy-start | bytes 3145732
  6.5 3.2 %copy-start.1 = (s32[32]{0:T(128)S(1)}, s32[32]{0:T(128)}, u32[]{:S(2)}) copy-start(s32[32]{0:T(128)} %param.25) | copy-start | bytes 388
  6.5 114.4 %all-gather.9.cloned.1.call-start = ((), (), s32[]{:S(2)}) async-start(), calls=%async_computation.3 | async-start | bytes 2359296 | tf_op jit(solution)/shard_map/all_gather | solution.py:63
  7.3 116.6 %all-gather.5.cloned.1.call-start = ((), (), s32[]{:S(2)}) async-start(), calls=%async_computation.1 | async-start | bytes 2359296 | tf_op jit(solution)/shard_map/all_gather | solution.py:64
  8.0 118.7 %all-gather.7.cloned.1.call-start = ((), (), s32[]{:S(2)}) async-start(), calls=%async_computation.2 | async-start | bytes 2359296 | tf_op jit(solution)/shard_map/all_gather | solution.py:62
  9.7 2.0 %copy-start.6 = (s32[32]{0:T(128)S(1)}, s32[32]{0:T(128)}, u32[]{:S(2)}) copy-start(s32[32]{0:T(128)} %param.24) | copy-start | bytes 388
  9.7 2.3 %copy-start.5 = (s32[32,8]{0,1:T(8,128)S(1)}, s32[32,8]{0,1:T(8,128)}, u32[]{:S(2)}) copy-start(s32[32,8]{0,1:T(8,128)} %param.23) | copy-start | bytes 3076
  19.6 1.4 copy-start.2
  22.2 18.1 %collective-permute-start = (bf16[1,128,1024]{2,1,0:T(8,128)(2,1)}, bf16[1,128,1024]{2,1,0:T(8,128)(2,1)}, u32[]{:S(2)}, u32[]{:S(2)}) collective-permute-start(bf16[1,128,1024]{2,1,0:T(8,128)(2,1)} %get-tuple-element.19), channel_id=1, source_target_pairs={{0,1},{1,2},{2,3},{3,4},{4,5},{5,6},{6,7},{7,0},{8,9},{9,10},{10,1... | collective-permute-start | bytes 786440 | tf_op jit(solution)/shard_map/ppermute | solution.py:27
  22.7 22.3 %collective-permute-start.1 = (bf16[1,128,1024]{2,1,0:T(8,128)(2,1)}, bf16[1,128,1024]{2,1,0:T(8,128)(2,1)}, u32[]{:S(2)}, u32[]{:S(2)}) collective-permute-start(bf16[1,128,1024]{2,1,0:T(8,128)(2,1)} %get-tuple-element.18), channel_id=1, source_target_pairs={{0,2},{1,3},{2,4},{3,5},{4,6},{5,7},{6,0},{7,1},{8,10},{9,11},{10,... | collective-permute-start | bytes 786440 | tf_op jit(solution)/shard_map/ppermute | solution.py:27
  25.3 24.1 %collective-permute-start.2 = (bf16[1,128,1024]{2,1,0:T(8,128)(2,1)}, bf16[1,128,1024]{2,1,0:T(8,128)(2,1)}, u32[]{:S(2)}, u32[]{:S(2)}) collective-permute-start(bf16[1,128,1024]{2,1,0:T(8,128)(2,1)} %get-tuple-element.17), channel_id=1, source_target_pairs={{0,3},{1,4},{2,5},{3,6},{4,7},{5,0},{6,1},{7,2},{8,11},{9,12},{10,... | collective-permute-start | bytes 786440 | tf_op jit(solution)/shard_map/ppermute | solution.py:27
  27.7 23.3 %collective-permute-start.3 = (bf16[1,128,1024]{2,1,0:T(8,128)(2,1)}, bf16[1,128,1024]{2,1,0:T(8,128)(2,1)}, u32[]{:S(2)}, u32[]{:S(2)}) collective-permute-start(bf16[1,128,1024]{2,1,0:T(8,128)(2,1)} %get-tuple-element.16), channel_id=1, source_target_pairs={{0,4},{1,5},{2,6},{3,7},{4,0},{5,1},{6,2},{7,3},{8,12},{9,13},{10,... | collective-permute-start | bytes 786440 | tf_op jit(solution)/shard_map/ppermute | solution.py:27
  28.2 32.6 %collective-permute-start.4 = (bf16[1,128,1024]{2,1,0:T(8,128)(2,1)}, bf16[1,128,1024]{2,1,0:T(8,128)(2,1)S(1)}, u32[]{:S(2)}, u32[]{:S(2)}) collective-permute-start(bf16[1,128,1024]{2,1,0:T(8,128)(2,1)} %get-tuple-element.15), channel_id=1, source_target_pairs={{0,5},{1,6},{2,7},{3,0},{4,1},{5,2},{6,3},{7,4},{8,13},{9,14},{10,... | collective-permute-start | bytes 786440 | tf_op jit(solution)/shard_map/ppermute | solution.py:27
  28.3 59.0 %all-to-all-start = ((bf16[8,128,1024]{2,1,0:T(8,128)(2,1)}), bf16[8,128,1024]{2,1,0:T(8,128)(2,1)S(1)}, u32[]{:S(2)}, u32[]{:S(2)}) async-start(bf16[8,128,1024]{2,1,0:T(8,128)(2,1)} %get-tuple-element.29), calls=%async_computation | async-start | bytes 4194304 | tf_op jit(solution)/shard_map/all_to_all | solution.py:91
  32.2 117.4 %all-gather.11.cloned.1.call-start = ((), (), s32[]{:S(2)}) async-start(), calls=%async_computation.4 | async-start | bytes 2359296 | tf_op jit(solution)/shard_map/all_gather | solution.py:155
  40.4 36.0 %collective-permute-start.5 = (bf16[1,128,1024]{2,1,0:T(8,128)(2,1)}, bf16[1,128,1024]{2,1,0:T(8,128)(2,1)S(1)}, u32[]{:S(2)}, u32[]{:S(2)}) collective-permute-start(bf16[1,128,1024]{2,1,0:T(8,128)(2,1)} %get-tuple-element.14), channel_id=1, source_target_pairs={{0,6},{1,7},{2,0},{3,1},{4,2},{5,3},{6,4},{7,5},{8,14},{9,15},{10,... | collective-permute-start | bytes 786440 | tf_op jit(solution)/shard_map/ppermute | solution.py:27
  45.0 36.1 %collective-permute-start.6 = (bf16[1,128,1024]{2,1,0:T(8,128)(2,1)}, bf16[1,128,1024]{2,1,0:T(8,128)(2,1)S(1)}, u32[]{:S(2)}, u32[]{:S(2)}) collective-permute-start(bf16[1,128,1024]{2,1,0:T(8,128)(2,1)} %get-tuple-element.13), channel_id=1, source_target_pairs={{0,7},{1,0},{2,1},{3,2},{4,3},{5,4},{6,5},{7,6},{8,15},{9,8},{10,9... | collective-permute-start | bytes 786440 | tf_op jit(solution)/shard_map/ppermute | solution.py:27
  89.8 17.4 %collective-permute-start.7 = (bf16[2,128,1024]{2,1,0:T(8,128)(2,1)}, bf16[2,128,1024]{2,1,0:T(8,128)(2,1)}, u32[]{:S(2)}, u32[]{:S(2)}) collective-permute-start(bf16[2,128,1024]{2,1,0:T(8,128)(2,1)} %pad_maximum_fusion), channel_id=1, source_target_pairs={{24,0},{0,8},{8,16},{16,24},{25,1},{1,9},{9,17},{17,25},{26,2},{2,... | collective-permute-start | bytes 1572872 | tf_op jit(solution)/shard_map/ppermute | solution.py:35
  96.4 21.4 %collective-permute-start.8 = (bf16[2,128,1024]{2,1,0:T(8,128)(2,1)}, bf16[2,128,1024]{2,1,0:T(8,128)(2,1)}, u32[]{:S(2)}, u32[]{:S(2)}) collective-permute-start(bf16[2,128,1024]{2,1,0:T(8,128)(2,1)} %pad_maximum_fusion.1), channel_id=1, source_target_pairs={{8,0},{16,8},{24,16},{0,24},{9,1},{17,9},{25,17},{1,25},{10,2},{18... | collective-permute-start | bytes 1572872 | tf_op jit(solution)/shard_map/ppermute | solution.py:35
  108.2 12.8 %copy-start.3 = (bf16[128,1024]{1,0:T(8,128)(2,1)S(1)}, bf16[128,1024]{1,0:T(8,128)(2,1)}, u32[]{:S(2)}) copy-start(bf16[128,1024]{1,0:T(8,128)(2,1)} %param.15) | copy-start | bytes 786436
  128.8 5.0 %copy-start.4 = (bf16[1,768,8,128]{1,3,2,0:T(8,128)(2,1)S(1)}, bf16[1,768,8,128]{1,3,2,0:T(8,128)(2,1)}, u32[]{:S(2)}) copy-start(bf16[1,768,8,128]{1,3,2,0:T(8,128)(2,1)} %copy.68) | copy-start | bytes 4718596
Sparse Core Ops, SparseCore 0:
  9.2 41.9 all-gather.8
  53.1 35.3 all-gather.4
  90.4 29.2 all-gather.6
  121.4 28.0 all-gather.10
